TPU v7x, 512 devices: a whole 4x4x16 slice. The times are simulated.
512 devices in a mesh: dp: 4 (over x), expert: 8 (over y, core), tensor: 16 (over z).
Axes of the slice: x: 4, y: 4, z: 16, core: 2. Of those that a mesh axis runs over, the one named last changes fastest.
Arguments:
- tokens: bfloat16 [2048, 3072], P('expert', 'dp'), may hold values from -6 to 6
- route_ids: int32 [2048, 2], P('expert'), may hold values from 0 to 7, all different within a row; in each aligned block of 256 rows (0 to 255, 256 to 511, ...) at most 96 rows name the same one
- gates: float32 [2048, 2], P('expert'), may hold values from 0.2 to 1
- w_gate: bfloat16 [8, 3072, 8192], P('expert', 'dp', 'tensor'), may hold values from -0.109375 to 0.109375
- w_up: bfloat16 [8, 3072, 8192], P('expert', 'dp', 'tensor'), may hold values from -0.109375 to 0.109375
- w_down: bfloat16 [8, 8192, 3072], P('expert', 'tensor', 'dp'), may hold values from -0.0625 to 0.0625
Outputs:
- mixed: bfloat16 [2048, 3072], P('expert', 'dp')
Inputs may be any that keep to these rules, and one draw needn't show every extreme that they name: `route_ids`: each token names two different experts. Among the 256 tokens of one index of expert, no expert is named by more than 96 tokens, a bound that some block reaches.
All inputs are finite; a program needn't handle non-finite values.
Results may differ from a plain program's by a relative error of at most 0.025.
Values may be sent and summed in bfloat16 or wider, within the bound.
A program may use at most 64 MiB of HBM per device.

v0:
```python
import jax
import jax.numpy as jnp
from jax import lax
from jax.sharding import PartitionSpec as P


def cut_along(value, dim, size):
    lengths = value.shape
    pieces = value.reshape(*lengths[:dim], size, lengths[dim] // size, *lengths[dim + 1 :])
    return jnp.moveaxis(pieces, dim, 0)


def sum_at_owner(value, axis, dim):
    pieces = cut_along(value, dim, lax.axis_size(axis))
    arrived = lax.all_to_all(pieces, axis, split_axis=0, concat_axis=0, tiled=True)
    return arrived.astype(jnp.float32).sum(axis=0)


def joined_along(pieces, dim):
    lengths = list(pieces.shape[1:])
    lengths[dim] *= pieces.shape[0]
    return jnp.moveaxis(pieces, 0, dim).reshape(lengths)


def copy_for_each(value, axis):
    size = lax.axis_size(axis)
    return lax.all_to_all(
        jnp.broadcast_to(value[None], (size, *value.shape)), axis, 0, 0, tiled=True
    )


def gather_directly(value, axis, dim):
    return joined_along(copy_for_each(value, axis), dim)


def slot_index(route_group, experts):
    flat = route_group.reshape(-1)
    hits = (flat[:, None] == jnp.arange(experts, dtype=jnp.int32)[None, :]).astype(jnp.int32)
    before = jnp.cumsum(hits, axis=0) - hits
    rank = jnp.sum(before * hits, axis=1)
    return (rank * experts + flat).reshape(-1, 2)


def activate(summed, hidden_units):
    return (jax.nn.silu(summed[..., :hidden_units]) * summed[..., hidden_units:]).astype(
        jnp.bfloat16
    )


def local(tokens, route_ids, gates, w_gate, w_up, w_down):
    experts = lax.axis_size("expert")
    tensor_devices = lax.axis_size("tensor")
    tok_rows = tokens.shape[0]
    width = tokens.shape[1]
    hidden_units = w_gate.shape[2]
    capacity = max(3 * tok_rows // 8, 2 * tok_rows // experts)
    capacity = (capacity + 15) // 16 * 16
    share_slots = capacity // tensor_devices
    places = slot_index(route_ids, experts)
    lines = 0 * experts + jnp.arange(capacity * experts, dtype=jnp.int32)
    chosen = (lines[:, None] == places[None, :, 0]) | (lines[:, None] == places[None, :, 1])
    picked = jnp.dot(chosen.astype(jnp.bfloat16), tokens, preferred_element_type=jnp.float32)
    received = lax.all_to_all(
        picked.astype(jnp.bfloat16).reshape(capacity, experts, width),
        "expert",
        split_axis=1,
        concat_axis=1,
        tiled=True,
    )
    rows = received.reshape(capacity * experts, width)
    gate_part = jnp.dot(rows, w_gate[0], preferred_element_type=jnp.float32).astype(jnp.bfloat16)
    up_part = jnp.dot(rows, w_up[0], preferred_element_type=jnp.float32).astype(jnp.bfloat16)
    both = jnp.concatenate([gate_part, up_part], axis=1)
    summed = sum_at_owner(both.reshape(capacity, experts, 2 * hidden_units), "dp", 0)
    hidden = lax.all_gather(activate(summed, hidden_units), "dp", axis=0, tiled=True)
    piece = hidden.reshape(share_slots * lax.axis_size("tensor") * experts, hidden_units)
    result = jnp.dot(piece, w_down[0], preferred_element_type=jnp.float32)
    finished = sum_at_owner(
        result.reshape(share_slots * lax.axis_size("tensor"), experts, width).astype(jnp.bfloat16),
        "tensor",
        0,
    ).astype(jnp.bfloat16)
    returned_share = lax.all_to_all(finished, "expert", split_axis=1, concat_axis=1, tiled=True)
    returned = gather_directly(returned_share, "tensor", 0)
    table = returned.reshape(capacity * experts, width)
    first_rows = table[places[:, 0]].astype(jnp.float32)
    second_rows = table[places[:, 1]].astype(jnp.float32)
    mixed = gates[:, 0:1] * first_rows + gates[:, 1:2] * second_rows
    return mixed.astype(jnp.bfloat16)


def solution(mesh):
    return jax.shard_map(
        local,
        mesh=mesh,
        in_specs=(
            P("expert", "dp"),
            P("expert", None),
            P("expert", None),
            P("expert", "dp", "tensor"),
            P("expert", "dp", "tensor"),
            P("expert", "tensor", "dp"),
        ),
        out_specs=P("expert", "dp"),
        check_vma=False,
    )
```

profile of v0, /device:TPU:32, one launch (start us, length us, event | category | flops | bytes accessed | tf_op | source)
XLA Modules:
  0.0 213.1 jit_solution(16417716052719693513)
XLA Ops:
  0.0 0.9 copy.28
  0.9 0.1 eq.60
  1.2 1.1 reduce-window.6
  2.4 0.2 slice_reduce_fusion.2
  2.9 0.3 fusion.13
  3.2 0.5 fusion
  3.7 0.2 copy.31
  3.9 21.8 %all_to_all.25 = bf16[96,8,768]{2,0,1:T(8,128)(2,1)S(1)} all-to-all(bf16[96,8,768]{2,0,1:T(8,128)(2,1)S(1)} %copy.31), channel_id=1, replica_groups=mesh['dp'=4,'expert'=8,'tensor'=16] {'expert'}, dimensions={1} | all-to-all | bytes 2359296 | tf_op jit(solution)/shard_map/all_to_all | solution.py:63
  25.7 1.2 convolution_convert_fusion.2
  26.9 1.2 convolution_convert_fusion.3
  28.2 1.7 copy.33
  29.8 24.8 %all_to_all.26 = bf16[4,24,8,1024]{3,2,1,0:T(8,128)(2,1)S(1)} all-to-all(bf16[4,24,8,1024]{3,2,1,0:T(8,128)(2,1)} %bitcast.34), channel_id=1, replica_groups=mesh['dp'=4,'expert'=8,'tensor'=16] {'dp'}, dimensions={0} | all-to-all | bytes 3145728 | tf_op jit(solution)/shard_map/all_to_all | solution.py:15
  54.6 0.3 convert_reduce_fusion
  55.1 14.0 %all_gather.3 = bf16[96,8,512]{2,1,0:T(8,128)(2,1)S(1)} all-gather(bf16[24,8,512]{2,1,0:T(8,128)(2,1)S(1)} %fusion.10), channel_id=1, replica_groups=mesh['dp'=4,'expert'=8,'tensor'=16] {'dp'}, dimensions={0}, use_global_device_ids=true | all-gather | bytes 983040 | tf_op jit(solution)/shard_map/all_gather | solution.py:75
  69.1 0.8 convolution_convert_fusion
  69.8 71.1 %all_to_all.27 = bf16[16,6,8,768]{3,2,1,0:T(8,128)(2,1)S(1)} all-to-all(bf16[16,6,8,768]{3,2,1,0:T(8,128)(2,1)S(1)} %bitcast.35), channel_id=1, replica_groups=mesh['dp'=4,'expert'=8,'tensor'=16] {'tensor'}, dimensions={0} | all-to-all | bytes 2359296 | tf_op jit(solution)/shard_map/all_to_all | solution.py:15
  140.9 0.2 reduce_sum.32
  141.1 8.2 %all_to_all.28 = bf16[6,8,768]{2,0,1:T(8,128)(2,1)S(1)} all-to-all(bf16[6,8,768]{2,0,1:T(8,128)(2,1)S(1)} %copy.34), channel_id=1, replica_groups=mesh['dp'=4,'expert'=8,'tensor'=16] {'expert'}, dimensions={1} | all-to-all | bytes 147456 | tf_op jit(solution)/shard_map/all_to_all | solution.py:83
  149.3 1.1 broadcast_in_dim.2
  150.4 4.1 %all-to-all-start.4 = ((bf16[16,6,8,768]{3,2,1,0:T(8,128)(2,1)}), bf16[16,6,8,768]{3,2,1,0:T(8,128)(2,1)S(1)}, u32[]{:S(2)}, u32[]{:S(2)}) async-start(bf16[16,6,8,768]{3,2,1,0:T(8,128)(2,1)} %broadcast_in_dim.2), calls=%async_computation.4 | async-start | bytes 2359296 | tf_op jit(solution)/shard_map/all_to_all | solution.py:27
  154.5 55.3 %all-to-all-done.4 = bf16[16,6,8,768]{3,2,1,0:T(8,128)(2,1)S(1)} async-done(((bf16[16,6,8,768]{3,2,1,0:T(8,128)(2,1)}), bf16[16,6,8,768]{3,2,1,0:T(8,128)(2,1)S(1)}, u32[]{:S(2)}, u32[]{:S(2)}) %all-to-all-start.4) | async-done | bytes 1179680 | tf_op jit(solution)/shard_map/all_to_all | solution.py:27
  209.8 1.2 gather_fusion
  211.0 1.2 gather_fusion.1
  212.2 1.0 add_convert_fusion
  (24 shorter events, 0.7 us)
Async XLA Ops:
  0.0 69.1 %copy-start = (bf16[1,512,768]{2,1,0:T(8,128)(2,1)S(1)}, bf16[1,512,768]{2,1,0:T(8,128)(2,1)}, u32[]{:S(2)}) copy-start(bf16[1,512,768]{2,1,0:T(8,128)(2,1)} %param.11) | copy-start | bytes 2359300
  0.0 3.2 %copy-start.1 = (bf16[256,768]{1,0:T(8,128)(2,1)S(1)}, bf16[256,768]{1,0:T(8,128)(2,1)}, u32[]{:S(2)}) copy-start(bf16[256,768]{1,0:T(8,128)(2,1)} %param.6) | copy-start | bytes 1179652
  3.9 21.8 %copy-start.3 = (bf16[1,768,512]{2,1,0:T(8,128)(2,1)S(1)}, bf16[1,768,512]{2,1,0:T(8,128)(2,1)}, u32[]{:S(2)}) copy-start(bf16[1,768,512]{2,1,0:T(8,128)(2,1)} %param.10) | copy-start | bytes 2359300
  25.7 1.2 copy-start.4
  150.4 4.1 %copy-start.2 = (f32[256,2]{0,1:T(2,128)S(1)}, f32[256,2]{0,1:T(2,128)}, u32[]{:S(2)}) copy-start(f32[256,2]{0,1:T(2,128)} %param.8) | copy-start | bytes 6148
  150.4 59.4 %all-to-all-start.4 = ((bf16[16,6,8,768]{3,2,1,0:T(8,128)(2,1)}), bf16[16,6,8,768]{3,2,1,0:T(8,128)(2,1)S(1)}, u32[]{:S(2)}, u32[]{:S(2)}) async-start(bf16[16,6,8,768]{3,2,1,0:T(8,128)(2,1)} %broadcast_in_dim.2), calls=%async_computation.4 | async-start | bytes 2359296 | tf_op jit(solution)/shard_map/all_to_all | solution.py:27
where the time goes:
time: 214 us; the launch traced here: 213 us
  blocking collectives  140 us (65%)
  waiting for transfers between devices  55.3 us (26%)
  local copies, waits for them, and re-layouts  6.93 us (3%)
  starting transfers between devices  4.08 us (2%)
  matrix products  3.62 us (2%)
  other arithmetic  3.2 us (1%)
    all_to_all x2, blocking collectives, sum_at_owner(): lax.all_to_all(pieces, axis, split_axis=0, concat_axis=0, tiled=True)  95.9 us
    all_to_all x1, waiting for transfers between devices, copy_for_each(): lax.all_to_all(jnp.broadcast_to(value[None], (size, *value.shape)), axis,...  55.3 us
    all_to_all x1, blocking collectives, local(): lax.all_to_all(picked.astype(jnp.bfloat16).reshape(capacity, experts, wid...  21.8 us
    all_gather x1, blocking collectives, local(): lax.all_gather(activate(summed, hidden_units), 'dp', axis=0, tiled=True)  14 us
    all_to_all x1, blocking collectives, local(): lax.all_to_all(finished, 'expert', split_axis=1, concat_axis=1, tiled=True)  8.18 us
  transfers between devices with their start and end apart: 1, of which 1 were waited for; matrix products, arithmetic and copies ran while one was open for 0% of the time, Pallas kernels for 0%

commit v1 on v0

v1 whole, which is shorter than its diff:
```python
import jax
import jax.numpy as jnp
from jax import lax
from jax.experimental import pallas as pl
from jax.experimental.pallas import tpu as pltpu
from jax.sharding import PartitionSpec as P

BF = jnp.bfloat16
F32 = jnp.float32
RING = 4
CAP = 96
ROWS = 2 * CAP
PART = ROWS // RING
NONE = -1000.0
NSEM = 110


def kernel(tok, route, gates, wg_h, wu_h, wd_h, out, *s):
    (wg, wu, wd, slots, pick, rows, dhop, part, rl, fin, cmb, hid, obuf, rhop, ret, gm, acc,
     zs, zrl, zfin, zcmb, ys, yrl, yfin, ycmb, zo, wsem, ssem, rsem, barrier_unused) = s
    width = tok.shape[1]
    tokens = tok.shape[0]
    x = lax.axis_index("dp")
    e = lax.axis_index("expert")
    z = lax.axis_index("tensor")
    y, c = lax.div(e, 2), lax.rem(e, 2)
    nz = RING * RING

    def chip(j):
        return lax.rem(y + j, RING)

    def dev_e(j, core):
        return {"expert": chip(j) * 2 + core}

    def dev_x(j):
        return {"dp": lax.rem(x + j, RING)}

    def dev_z(j):
        return {"tensor": lax.rem(z + nz + j, nz)}

    loads = [pltpu.make_async_copy(a, b, wsem.at[i])
             for i, (a, b) in enumerate(((wg_h, wg), (wu_h, wu), (wd_h, wd)))]
    for load in loads:
        load.start()

    barrier = pltpu.get_barrier_semaphore()
    peers = [dev_e(0, 1 - c)] + [dev_e(j, k) for j in (1, 3) for k in (0, 1)]
    peers += [dev_x(1), dev_x(3)] + [dev_z(j) for j in (1, -1, 4, -4)]
    for peer in peers:
        pl.semaphore_signal(barrier, inc=1, device_id=peer, device_id_type=pl.DeviceIdType.MESH)

    used = [0]
    pending = []

    def take(n=1):
        used[0] += n
        assert used[0] <= NSEM
        return used[0] - n

    def send(src, dst, dev, k, k_recv):
        copy = pltpu.make_async_remote_copy(
            src_ref=src, dst_ref=dst, send_sem=ssem.at[k], recv_sem=rsem.at[k_recv],
            device_id=dev, device_id_type=pl.DeviceIdType.MESH)
        copy.start()
        pending.append(copy)
        return copy

    def arrived(dst, k):
        pltpu.make_async_remote_copy(
            src_ref=dst, dst_ref=dst, send_sem=ssem.at[0], recv_sem=rsem.at[k],
            device_id=dev_e(0, 1 - c), device_id_type=pl.DeviceIdType.MESH).wait_recv()

    r0, r1 = route[:, 0:1], route[:, 1:2]
    lane = lax.broadcasted_iota(jnp.int32, (tokens, 128), 1)
    hit0, hit1 = lane == r0, lane == r1
    hits = jnp.where(hit0 | hit1, 1.0, 0.0)
    earlier = jnp.where(
        lax.broadcasted_iota(jnp.int32, (tokens, tokens), 1)
        < lax.broadcasted_iota(jnp.int32, (tokens, tokens), 0), 1.0, 0.0)
    rank = jnp.dot(earlier.astype(BF), hits.astype(BF), preferred_element_type=F32)
    slots[...] = jnp.where(hit0 | hit1, rank, NONE).T

    def picked(j):
        line = lax.broadcasted_iota(jnp.int32, (ROWS, tokens), 0).astype(F32)
        first = slots[pl.ds(chip(j) * 2, 1), :]
        second = slots[pl.ds(chip(j) * 2 + 1, 1), :] + float(CAP)
        chosen = jnp.where((line == first) | (line == second), 1.0, 0.0).astype(BF)
        got = jnp.dot(chosen, tok[...], preferred_element_type=F32).astype(BF)
        pick[j] = got.reshape(2, CAP, width)

    half = CAP // 2
    ks_d = {j: take(2) for j in (1, 3)}
    k_dhop = take(2)
    k_fwd = {1: take(2), 3: take(2)}
    k_own = take()

    picked(2)
    pl.semaphore_wait(barrier, len(peers))
    send(pick.at[2, :, 0:half], dhop.at[0], dev_e(1, c), k_dhop, k_dhop)
    send(pick.at[2, :, half:CAP], dhop.at[1], dev_e(3, c), k_dhop + 1, k_dhop + 1)
    for j in (1, 3):
        picked(j)
        for core in (0, 1):
            send(pick.at[j, core], rows.at[RING - j, c], dev_e(j, core), ks_d[j] + core, ks_d[j] + c)
    picked(0)
    send(pick.at[0, 1 - c], rows.at[0, c], dev_e(0, 1 - c), k_own, k_own)
    rows[0, c] = pick[0, c]

    def dispatch_forward():
        arrived(dhop.at[0], k_dhop)
        for core in (0, 1):
            send(dhop.at[0, core], rows.at[2, c, 0:half], dev_e(1, core), k_fwd[1] + core, k_fwd[1] + c)
        arrived(dhop.at[1], k_dhop + 1)
        for core in (0, 1):
            send(dhop.at[1, core], rows.at[2, c, half:CAP], dev_e(3, core), k_fwd[3] + core, k_fwd[3] + c)

    def rows_here(j):
        if j == 0:
            arrived(rows.at[0, 1 - c], k_own)
        elif j == 2:
            for core in (0, 1):
                arrived(rows.at[2, core, 0:half], k_fwd[1] + core)
                arrived(rows.at[2, core, half:CAP], k_fwd[3] + core)
        else:
            for core in (0, 1):
                arrived(rows.at[j, core], ks_d[RING - j] + core)

    def rs_start(own, i, left, right, relay, done):
        k = take(6)
        opp, r, l = lax.rem(i + 2, RING), lax.rem(i + 1, RING), lax.rem(i + 3, RING)
        send(own.at[0, opp], relay.at[0], right, k, k)
        send(own.at[1, opp], relay.at[1], left, k + 1, k + 1)
        send(own.at[1, r], done.at[0], right, k + 2, k + 2)
        send(own.at[0, l], done.at[1], left, k + 3, k + 3)
        return k

    def rs_relay(k, own, i, left, right, relay, done, mixed):
        r, l = lax.rem(i + 1, RING), lax.rem(i + 3, RING)
        arrived(relay.at[0], k)
        mixed[0] = (own[0, r].astype(F32) + relay[0].astype(F32)).astype(BF)
        send(mixed.at[0], done.at[2], right, k + 4, k + 4)
        arrived(relay.at[1], k + 1)
        mixed[1] = (own[1, l].astype(F32) + relay[1].astype(F32)).astype(BF)
        send(mixed.at[1], done.at[3], left, k + 5, k + 5)

    def rs_finish(k, own, i, done):
        for n in range(4):
            arrived(done.at[n], k + 2 + n)
        first = own[0, i].astype(F32) + done[1].astype(F32) + done[2].astype(F32)
        second = own[1, i].astype(F32) + done[0].astype(F32) + done[3].astype(F32)
        return first, second

    def ag_start(at, i, left, right):
        k = take(6)
        send(at(0, i), at(0, i), right, k, k)
        send(at(1, i), at(1, i), left, k + 1, k + 1)
        send(at(1, i), at(1, i), right, k + 2, k + 2)
        send(at(0, i), at(0, i), left, k + 3, k + 3)
        return k

    def ag_relay(k, at, i, left, right):
        r, l = lax.rem(i + 1, RING), lax.rem(i + 3, RING)
        arrived(at(0, l), k)
        send(at(0, l), at(0, l), right, k + 4, k + 4)
        arrived(at(1, r), k + 1)
        send(at(1, r), at(1, r), left, k + 5, k + 5)

    def ag_finish(k, at, i):
        opp, r, l = lax.rem(i + 2, RING), lax.rem(i + 1, RING), lax.rem(i + 3, RING)
        arrived(at(1, l), k + 2)
        arrived(at(0, r), k + 3)
        arrived(at(0, opp), k + 4)
        arrived(at(1, opp), k + 5)

    xl, xr = dev_x(3), dev_x(1)
    rs_k, ag_k = {}, {}

    def hid_at(j):
        return lambda h, i: hid.at[j, h, i]

    def G(j):
        rows_here(j)
        if j == 0:
            loads[0].wait()
            loads[1].wait()
        here = rows[j].reshape(ROWS, width)
        for n, w in enumerate((wg, wu)):
            got = jnp.dot(here, w[...], preferred_element_type=F32).astype(BF)
            part[j, n] = got.reshape(RING, PART, got.shape[1])
        rs_k[j] = rs_start(part.at[j], x, xl, xr, rl.at[j], fin.at[j])

    def R(j):
        rs_relay(rs_k[j], part.at[j], x, xl, xr, rl.at[j], fin.at[j], cmb.at[j])

    def H(j):
        gate, up = rs_finish(rs_k[j], part.at[j], x, fin.at[j])
        got = (gate / (1.0 + jnp.exp(-gate)) * up).astype(BF)
        hw = got.shape[1] // 2
        hid[j, 0, x] = got[:, :hw]
        hid[j, 1, x] = got[:, hw:]
        ag_k[j] = ag_start(hid_at(j), x, xl, xr)

    def F(j):
        ag_relay(ag_k[j], hid_at(j), x, xl, xr)

    k_ret = {j: take(2) for j in (1, 3)}
    k_rhop = take(2)
    k_rfwd = {1: take(2), 3: take(2)}
    k_rown = take()

    def O(j, first_use=False):
        ag_finish(ag_k[j], hid_at(j), x)
        if first_use:
            loads[2].wait()
        hw = wd.shape[0] // 2
        got = jnp.dot(hid[j, 0].reshape(ROWS, hw), wd[0:hw], preferred_element_type=F32)
        got += jnp.dot(hid[j, 1].reshape(ROWS, hw), wd[hw:], preferred_element_type=F32)
        obuf[j] = got.astype(BF).reshape(2, CAP, width)
        if j == 0:
            send(obuf.at[0, 1 - c], ret.at[0, c], dev_e(0, 1 - c), k_rown, k_rown)
            ret[0, c] = obuf[0, c]
        elif j == 2:
            send(obuf.at[2, :, 0:half], rhop.at[0], dev_e(1, c), k_rhop, k_rhop)
            send(obuf.at[2, :, half:CAP], rhop.at[1], dev_e(3, c), k_rhop + 1, k_rhop + 1)
        else:
            for core in (0, 1):
                send(obuf.at[j, core], ret.at[RING - j, c], dev_e(j, core), k_ret[j] + core, k_ret[j] + c)

    def return_forward():
        arrived(rhop.at[0], k_rhop)
        for core in (0, 1):
            send(rhop.at[0, core], ret.at[2, c, 0:half], dev_e(1, core), k_rfwd[1] + core, k_rfwd[1] + c)
        arrived(rhop.at[1], k_rhop + 1)
        for core in (0, 1):
            send(rhop.at[1, core], ret.at[2, c, half:CAP], dev_e(3, core), k_rfwd[3] + core, k_rfwd[3] + c)

    def combine_table():
        ranks = jnp.where(hit0, rank, 0.0), jnp.where(hit1, rank, 0.0)
        places = [jnp.sum(v, axis=1, keepdims=True) + r.astype(F32) * float(CAP)
                  for v, r in zip(ranks, (r0, r1))]
        column = lax.broadcasted_iota(jnp.int32, (tokens, ROWS), 1)
        for j in range(RING):
            here = (column + chip(j) * ROWS).astype(F32)
            weight = jnp.where(here == places[0], gates[:, 0:1], 0.0)
            weight += jnp.where(here == places[1], gates[:, 1:2], 0.0)
            gm[j] = weight.astype(BF)

    def C(j, first=False):
        if j == 0:
            arrived(ret.at[0, 1 - c], k_rown)
        elif j == 2:
            for core in (0, 1):
                arrived(ret.at[2, core, 0:half], k_rfwd[1] + core)
                arrived(ret.at[2, core, half:CAP], k_rfwd[3] + core)
        else:
            for core in (0, 1):
                arrived(ret.at[j, core], k_ret[RING - j] + core)
        got = jnp.dot(gm[j], ret[j].reshape(ROWS, width), preferred_element_type=F32)
        if first:
            acc[...] = got
        else:
            acc[...] += got

    G(0)
    dispatch_forward()
    R(0)
    combine_table()
    H(0)
    G(1)
    G(3)
    F(0)
    R(1)
    R(3)
    O(0, True)
    H(1)
    H(3)
    G(2)
    F(1)
    F(3)
    R(2)
    O(1)
    O(3)
    C(0, True)
    H(2)
    F(2)
    O(2)
    C(1)
    C(3)
    return_forward()
    C(2)

    za, zb = lax.rem(z, RING), lax.div(z, RING)
    cols = width // 2
    block = tokens // RING
    sub = block // RING
    for h in range(2):
        zs[h] = acc[:, h * cols:(h + 1) * cols].astype(BF).reshape(RING, block, cols)
    zl, zr = dev_z(-1), dev_z(1)
    k = rs_start(zs, za, zl, zr, zrl, zfin)
    rs_relay(k, zs, za, zl, zr, zrl, zfin, zcmb)
    for h, v in enumerate(rs_finish(k, zs, za, zfin)):
        ys[h] = v.astype(BF).reshape(RING, sub, cols)
    yl, yr = dev_z(-4), dev_z(4)
    k = rs_start(ys, zb, yl, yr, yrl, yfin)
    rs_relay(k, ys, zb, yl, yr, yrl, yfin, ycmb)
    for h, v in enumerate(rs_finish(k, ys, zb, yfin)):
        zo[h, za, zb] = v.astype(BF)

    def far(h, i):
        return zo.at[h, za, i]

    def near(h, i):
        return zo.at[h, i]

    k = ag_start(far, zb, yl, yr)
    ag_relay(k, far, zb, yl, yr)
    ag_finish(k, far, zb)
    k = ag_start(near, za, zl, zr)
    ag_relay(k, near, za, zl, zr)
    ag_finish(k, near, za)
    for h in range(2):
        out[:, h * cols:(h + 1) * cols] = zo[h].reshape(tokens, cols)
    for copy in pending:
        copy.wait_send()


def local(tokens, route_ids, gates, w_gate, w_up, w_down):
    w_gate, w_up, w_down = w_gate[0], w_up[0], w_down[0]
    n, width = tokens.shape
    units = w_gate.shape[1]
    cols, block = width // 2, n // RING
    sub = block // RING
    V = pltpu.VMEM
    scratch = [
        V(w_gate.shape, BF), V(w_up.shape, BF), V(w_down.shape, BF),
        V((128, n), F32),
        V((RING, 2, CAP, width), BF),
        V((RING, 2, CAP, width), BF),
        V((2, 2, CAP // 2, width), BF),
        V((RING, 2, RING, PART, units), BF),
        V((RING, 2, PART, units), BF),
        V((RING, 4, PART, units), BF),
        V((RING, 2, PART, units), BF),
        V((RING, 2, RING, PART, units // 2), BF),
        V((RING, 2, CAP, width), BF),
        V((2, 2, CAP // 2, width), BF),
        V((RING, 2, CAP, width), BF),
        V((RING, n, ROWS), BF),
        V((n, width), F32),
        V((2, RING, block, cols), BF),
        V((2, block, cols), BF),
        V((4, block, cols), BF),
        V((2, block, cols), BF),
        V((2, RING, sub, cols), BF),
        V((2, sub, cols), BF),
        V((4, sub, cols), BF),
        V((2, sub, cols), BF),
        V((2, RING, RING, sub, cols), BF),
        pltpu.SemaphoreType.DMA((3,)),
        pltpu.SemaphoreType.DMA((NSEM,)),
        pltpu.SemaphoreType.DMA((NSEM,)),
        pltpu.SemaphoreType.REGULAR,
    ]
    vmem = pl.BlockSpec(memory_space=pltpu.VMEM)
    anyspace = pl.BlockSpec(memory_space=pl.ANY)
    return pl.pallas_call(
        kernel,
        out_shape=jax.ShapeDtypeStruct((n, width), BF),
        in_specs=[vmem, vmem, vmem, anyspace, anyspace, anyspace],
        out_specs=vmem,
        scratch_shapes=scratch,
        compiler_params=pltpu.CompilerParams(
            collective_id=0, has_side_effects=True, vmem_limit_bytes=48 * 1024 * 1024),
        name="expert_layer",
    )(tokens, route_ids, gates, w_gate, w_up, w_down)


def solution(mesh):
    return jax.shard_map(
        local,
        mesh=mesh,
        in_specs=(
            P("expert", "dp"),
            P("expert", None),
            P("expert", None),
            P("expert", "dp", "tensor"),
            P("expert", "dp", "tensor"),
            P("expert", "tensor", "dp"),
        ),
        out_specs=P("expert", "dp"),
        check_vma=False,
    )
```

time: 214 us -> 103 us (0.48)
  the two profiles are of different devices: /device:TPU:32 before, /device:TPU:46 now
where the time goes in v1:
time: 103 us; the launch traced here: 102 us
  Pallas kernels  95.5 us (93%)
  local copies, waits for them, and re-layouts  6.63 us (6%)
    pallas_call x1, Pallas kernels, local(): pl.pallas_call(kernel, out_shape=jax.ShapeDtypeStruct((n, width), BF), in...  95.5 us
    unnamed x15, local copies, waits for them, and re-layouts  6.63 us

profile of v1, /device:TPU:46, one launch (start us, length us, event | category | flops | bytes accessed | tf_op | source)
XLA Modules:
  0.0 102.2 jit_solution(12458012069551922953)
XLA Ops:
  0.0 0.0 copy-start.4
  0.0 0.7 copy-done.4
  0.7 0.0 copy-start.5
  0.7 0.1 copy.7.route
  0.8 0.5 copy-done.5
  1.4 0.1 copy.8.gates
  1.5 0.0 copy-start
  1.5 1.1 %copy-done = bf16[1,768,512]{2,1,0:T(8,128)(2,1)S(1)} copy-done((bf16[1,768,512]{2,1,0:T(8,128)(2,1)S(1)}, bf16[1,768,512]{2,1,0:T(8,128)(2,1)}, u32[]{:S(2)}) %copy-start) | copy-done | bytes 786456
  2.6 0.0 copy-start.1
  2.6 1.1 %copy-done.1 = bf16[1,768,512]{2,1,0:T(8,128)(2,1)S(1)} copy-done((bf16[1,768,512]{2,1,0:T(8,128)(2,1)S(1)}, bf16[1,768,512]{2,1,0:T(8,128)(2,1)}, u32[]{:S(2)}) %copy-start.1) | copy-done | bytes 786456
  3.8 0.0 copy-start.2
  3.8 1.1 %copy-done.2 = bf16[1,512,768]{2,1,0:T(8,128)(2,1)S(1)} copy-done((bf16[1,512,768]{2,1,0:T(8,128)(2,1)S(1)}, bf16[1,512,768]{2,1,0:T(8,128)(2,1)}, u32[]{:S(2)}) %copy-start.2) | copy-done | bytes 786456
  4.9 0.0 copy-start.3
  4.9 1.0 copy-done.3
  5.9 95.5 %expert_layer.1 = bf16[256,768]{1,0:T(8,128)(2,1)S(1)} custom-call(bf16[256,768]{1,0:T(8,128)(2,1)S(1)} %copy-done.3, s32[256,2]{1,0:T(8,128)S(1)} %copy.7.route, f32[256,2]{1,0:T(8,128)S(1)} %copy.8.gates, bf16[768,512]{1,0:T(8,128)(2,1)S(1)} %bitcast.3, bf16[768,512]{1,0:T(8,128)(2,1)S(1)} %bitcast.4, bf16[512,768]{1,0:T(8,128)(2,1)S(1)} %bitcast.5), custom_call_target="tpu_custom_call" | custom-call | tf_op jit(solution)/shard_map/expert_layer/pallas_call | solution.py:366
  101.4 0.7 copy.10
Async XLA Ops:
  0.0 0.7 copy-start.4
  0.7 0.7 copy-start.5
  1.5 1.1 %copy-start = (bf16[1,768,512]{2,1,0:T(8,128)(2,1)S(1)}, bf16[1,768,512]{2,1,0:T(8,128)(2,1)}, u32[]{:S(2)}) copy-start(bf16[1,768,512]{2,1,0:T(8,128)(2,1)} %param.9) | copy-start | bytes 2359300
  2.6 1.1 %copy-start.1 = (bf16[1,768,512]{2,1,0:T(8,128)(2,1)S(1)}, bf16[1,768,512]{2,1,0:T(8,128)(2,1)}, u32[]{:S(2)}) copy-start(bf16[1,768,512]{2,1,0:T(8,128)(2,1)} %param.10) | copy-start | bytes 2359300
  3.8 1.1 %copy-start.2 = (bf16[1,512,768]{2,1,0:T(8,128)(2,1)S(1)}, bf16[1,512,768]{2,1,0:T(8,128)(2,1)}, u32[]{:S(2)}) copy-start(bf16[1,512,768]{2,1,0:T(8,128)(2,1)} %param.11) | copy-start | bytes 2359300
  4.9 1.0 copy-start.3

commit v2 on v1

v2 whole, which is shorter than its diff:
```python
import jax
import jax.numpy as jnp
from jax import lax
from jax.experimental import pallas as pl
from jax.experimental.pallas import tpu as pltpu
from jax.sharding import PartitionSpec as P

BF = jnp.bfloat16
F32 = jnp.float32
RING = 4
CAP = 96
ROWS = 2 * CAP
PART = ROWS // RING
NONE = -1000.0
NSEM = 190
QUARTER = CAP // RING


def kernel(tok_h, route, gates, wg_h, wu_h, wd_h, out, *s):
    (tok, wg, wu, wd, slots, table, pick, rows, farpick, far_rows, part, rl, fin, cmb, hid, obuf, far_out, rhop, ret,
     far_ret, gm, acc, *zbufs) = s[:-4]
    wsem, ssem, rsem, ready = s[-4:]
    tokens, width = tok.shape
    x = lax.axis_index("dp")
    e = lax.axis_index("expert")
    z = lax.axis_index("tensor")
    y, c = lax.div(e, 2), lax.rem(e, 2)
    nz = RING * RING

    def chip(j):
        return lax.rem(y + j, RING)

    def dev_e(j, core):
        return {"expert": chip(j) * 2 + core}

    def dev_x(j):
        return {"dp": lax.rem(x + j, RING)}

    def dev_z(j):
        return {"tensor": lax.rem(z + nz + j, nz)}

    loads = [pltpu.make_async_copy(a, b, wsem.at[i])
             for i, (a, b) in enumerate(((tok_h, tok), (wg_h, wg), (wu_h, wu), (wd_h, wd)))]
    for load in loads:
        load.start()

    barrier = pltpu.get_barrier_semaphore()
    peers = [dev_e(0, 1 - c)] + [dev_e(j, k) for j in (1, 2, 3) for k in (0, 1)]
    peers += [dev_x(1), dev_x(3)] + [dev_z(j) for j in (1, -1, 2, -2, 4, -4)]
    for peer in peers:
        pl.semaphore_signal(barrier, inc=1, device_id=peer, device_id_type=pl.DeviceIdType.MESH)

    used = [0]
    pending = []

    def take(n=1):
        used[0] += n
        assert used[0] <= NSEM
        return used[0] - n

    def send(src, dst, dev, k, k_recv):
        copy = pltpu.make_async_remote_copy(
            src_ref=src, dst_ref=dst, send_sem=ssem.at[k], recv_sem=rsem.at[k_recv],
            device_id=dev, device_id_type=pl.DeviceIdType.MESH)
        copy.start()
        pending.append(copy)
        return copy

    def arrived(dst, k):
        pltpu.make_async_remote_copy(
            src_ref=dst, dst_ref=dst, send_sem=ssem.at[0], recv_sem=rsem.at[k],
            device_id=dev_e(0, 1 - c), device_id_type=pl.DeviceIdType.MESH).wait_recv()

    r0, r1 = route[0:1, :], route[1:2, :]
    line = lax.broadcasted_iota(jnp.int32, (16, tokens), 0)
    hit0, hit1 = line == r0, line == r1
    hits = jnp.where(hit0 | hit1, 1.0, 0.0)
    later = jnp.where(
        lax.broadcasted_iota(jnp.int32, (tokens, tokens), 1)
        > lax.broadcasted_iota(jnp.int32, (tokens, tokens), 0), 1.0, 0.0)
    rank = jnp.dot(hits.astype(BF), later.astype(BF), preferred_element_type=F32)
    slots[...] = jnp.where(hit0 | hit1, rank, NONE)
    table[...] = jnp.zeros_like(table)
    for n, (hit, r) in enumerate(((hit0, r0), (hit1, r1))):
        place = jnp.sum(jnp.where(hit, rank, 0.0), axis=0, keepdims=True) + r.astype(F32) * float(CAP)
        table[n:n + 1, :] = place
        table[n + 2:n + 3, :] = gates[n:n + 1, :]

    def picked(j):
        line = lax.broadcasted_iota(jnp.int32, (ROWS, tokens), 0).astype(F32)
        first = slots[pl.ds(chip(j) * 2, 1), :]
        second = slots[pl.ds(chip(j) * 2 + 1, 1), :] + float(CAP)
        chosen = jnp.where((line == first) | (line == second), 1.0, 0.0).astype(BF)
        got = jnp.dot(chosen, tok[...], preferred_element_type=F32).astype(BF)
        pick[j] = got.reshape(2, CAP, width)

    ks_d = {j: take(2) for j in (1, 3)}
    k_far = take(2)
    k_spread = take(4)
    k_own = take()
    za, zb = lax.rem(z, RING), lax.div(z, RING)

    loads[0].wait()
    line = lax.broadcasted_iota(jnp.int32, (2 * QUARTER, tokens), 0)
    slot = jnp.where(line < QUARTER, line, line - QUARTER) + za * QUARTER
    place = jnp.where(line < QUARTER, slots[pl.ds(chip(2) * 2, 1), :], slots[pl.ds(chip(2) * 2 + 1, 1), :])
    chosen = jnp.where(slot.astype(F32) == place, 1.0, 0.0).astype(BF)
    got = jnp.dot(chosen, tok[...], preferred_element_type=F32).astype(BF)
    farpick[...] = got.reshape(2, QUARTER, width)
    pl.semaphore_wait(barrier, len(peers))
    for core in (0, 1):
        send(farpick.at[core], far_rows.at[za, c], dev_e(2, core), k_far + core, k_far + c)
    for j in (4, -4):
        pl.semaphore_signal(ready, inc=1, device_id=dev_z(j), device_id_type=pl.DeviceIdType.MESH)
    for j in (3, 1):
        picked(j)
        for core in (0, 1):
            send(pick.at[j, core], rows.at[RING - j, c], dev_e(j, core), ks_d[j] + core, ks_d[j] + c)
    picked(0)
    send(pick.at[0, 1 - c], rows.at[0, c], dev_e(0, 1 - c), k_own, k_own)
    rows[0, c] = pick[0, c]

    def far_spread():
        for core in (0, 1):
            arrived(far_rows.at[za, core], k_far + core)
        for n, j in enumerate((1, -1)):
            send(far_rows.at[za], far_rows.at[za], dev_z(j), k_spread + n, k_spread + n)
        for n, j in enumerate((2, -2)):
            send(far_rows.at[za, n], far_rows.at[za, n], dev_z(j), k_spread + 2 + n, k_spread + 2 + n)

    def rows_here(j):
        if j == 0:
            arrived(rows.at[0, 1 - c], k_own)
        elif j == 2:
            arrived(far_rows.at[lax.rem(za + 3, RING)], k_spread)
            arrived(far_rows.at[lax.rem(za + 1, RING)], k_spread + 1)
            for n in (0, 1):
                arrived(far_rows.at[lax.rem(za + 2, RING), n], k_spread + 2 + n)
        else:
            for core in (0, 1):
                arrived(rows.at[j, core], ks_d[RING - j] + core)

    def rs_start(own, i, left, right, bufs):
        k = take(6)
        relay, done, _ = bufs
        opp, r, l = lax.rem(i + 2, RING), lax.rem(i + 1, RING), lax.rem(i + 3, RING)
        send(own[0].at[opp], relay[0], right, k, k)
        send(own[1].at[opp], relay[1], left, k + 1, k + 1)
        send(own[1].at[r], done[0], right, k + 2, k + 2)
        send(own[0].at[l], done[1], left, k + 3, k + 3)
        return k

    def rs_relay(k, own, i, left, right, bufs):
        relay, done, mixed = bufs
        r, l = lax.rem(i + 1, RING), lax.rem(i + 3, RING)
        arrived(relay[0], k)
        mixed[0][...] = (own[0][r].astype(F32) + relay[0][...].astype(F32)).astype(BF)
        send(mixed[0], done[2], right, k + 4, k + 4)
        arrived(relay[1], k + 1)
        mixed[1][...] = (own[1][l].astype(F32) + relay[1][...].astype(F32)).astype(BF)
        send(mixed[1], done[3], left, k + 5, k + 5)

    def rs_finish(k, own, i, bufs):
        done = bufs[1]
        for n in range(4):
            arrived(done[n], k + 2 + n)
        first = own[0][i].astype(F32) + done[1][...].astype(F32) + done[2][...].astype(F32)
        second = own[1][i].astype(F32) + done[0][...].astype(F32) + done[3][...].astype(F32)
        return first, second

    def ag_start(at, i, left, right):
        k = take(6)
        send(at(0, i), at(0, i), right, k, k)
        send(at(1, i), at(1, i), left, k + 1, k + 1)
        send(at(1, i), at(1, i), right, k + 2, k + 2)
        send(at(0, i), at(0, i), left, k + 3, k + 3)
        return k

    def ag_relay(k, at, i, left, right):
        r, l = lax.rem(i + 1, RING), lax.rem(i + 3, RING)
        arrived(at(0, l), k)
        send(at(0, l), at(0, l), right, k + 4, k + 4)
        arrived(at(1, r), k + 1)
        send(at(1, r), at(1, r), left, k + 5, k + 5)

    def ag_finish(k, at, i):
        opp, r, l = lax.rem(i + 2, RING), lax.rem(i + 1, RING), lax.rem(i + 3, RING)
        arrived(at(1, l), k + 2)
        arrived(at(0, r), k + 3)
        arrived(at(0, opp), k + 4)
        arrived(at(1, opp), k + 5)

    xl, xr = dev_x(3), dev_x(1)
    rs_k, ag_k = {}, {}

    def xbufs(j):
        return ([rl.at[j, h] for h in range(2)], [fin.at[j, n] for n in range(4)],
                [cmb.at[j, h] for h in range(2)])

    def xown(j):
        return [part.at[j, h] for h in range(2)]

    def hid_at(j):
        return lambda h, i: hid.at[j, h, i]

    def G(j):
        rows_here(j)
        if j == 0:
            loads[1].wait()
            loads[2].wait()
        here = (far_rows if j == 2 else rows.at[j])[...].reshape(ROWS, width)
        for n, w in enumerate((wg, wu)):
            got = jnp.dot(here, w[...], preferred_element_type=F32).astype(BF)
            part[j, n] = got.reshape(RING, PART, got.shape[1])
        rs_k[j] = rs_start(xown(j), x, xl, xr, xbufs(j))

    def R(j):
        rs_relay(rs_k[j], xown(j), x, xl, xr, xbufs(j))

    def H(j):
        gate, up = rs_finish(rs_k[j], xown(j), x, xbufs(j))
        got = (gate / (1.0 + jnp.exp(-gate)) * up).astype(BF)
        hw = got.shape[1] // 2
        hid[j, 0, x] = got[:, :hw]
        hid[j, 1, x] = got[:, hw:]
        ag_k[j] = ag_start(hid_at(j), x, xl, xr)

    def F(j):
        ag_relay(ag_k[j], hid_at(j), x, xl, xr)

    k_ret = {j: take(2) for j in (1, 3)}
    k_rhop = take(4)
    k_rfwd = {1: take(4), 3: take(4)}
    k_rown = take()

    def O(j, first_use=False):
        ag_finish(ag_k[j], hid_at(j), x)
        if first_use:
            loads[3].wait()
        hw = wd.shape[0] // 2
        got = jnp.dot(hid[j, 0].reshape(ROWS, hw), wd[0:hw], preferred_element_type=F32)
        got += jnp.dot(hid[j, 1].reshape(ROWS, hw), wd[hw:], preferred_element_type=F32)
        got = got.astype(BF)
        if j == 2:
            far_out[...] = got.reshape(far_out.shape)
            for a in (0, 1):
                for n in (0, 1):
                    send(far_out.at[2 * n + a], rhop.at[n, a], dev_e(1 + 2 * n, c), k_rhop + 2 * n + a, k_rhop + 2 * n + a)
            return
        obuf[j] = got.reshape(2, CAP, width)
        if j == 0:
            send(obuf.at[0, 1 - c], ret.at[0, c], dev_e(0, 1 - c), k_rown, k_rown)
            ret[0, c] = obuf[0, c]
        else:
            for core in (0, 1):
                send(obuf.at[j, core], ret.at[RING - j, c], dev_e(j, core), k_ret[j] + core, k_ret[j] + c)

    def return_forward():
        for a in (0, 1):
            for n in (0, 1):
                arrived(rhop.at[n, a], k_rhop + 2 * n + a)
                k = k_rfwd[1 + 2 * n] + 2 * a
                for core in (0, 1):
                    send(rhop.at[n, a, core], far_ret.at[c, 2 * n + a], dev_e(1 + 2 * n, core), k + core, k + c)

    def combine_table():
        by_token = table[...].T
        column = lax.broadcasted_iota(jnp.int32, (tokens, ROWS), 1)
        for j in range(RING):
            here = (column + chip(j) * ROWS).astype(F32)
            weight = jnp.where(here == by_token[:, 0:1], by_token[:, 2:3], 0.0)
            weight += jnp.where(here == by_token[:, 1:2], by_token[:, 3:4], 0.0)
            gm[j] = weight.astype(BF)

    def C(j, first=False):
        if j == 0:
            arrived(ret.at[0, 1 - c], k_rown)
        elif j == 2:
            for a in (0, 1):
                for n in (0, 1):
                    for core in (0, 1):
                        arrived(far_ret.at[core, 2 * n + a], k_rfwd[1 + 2 * n] + 2 * a + core)
        else:
            for core in (0, 1):
                arrived(ret.at[j, core], k_ret[RING - j] + core)
        back = (far_ret if j == 2 else ret.at[j])[...].reshape(ROWS, width)
        got = jnp.dot(gm[j], back, preferred_element_type=F32)
        if first:
            acc[...] = got
        else:
            acc[...] += got

    G(0)
    combine_table()
    R(0)
    far_spread()
    H(0)
    G(1)
    G(3)
    F(0)
    R(1)
    R(3)
    G(2)
    O(0, True)
    H(1)
    R(2)
    H(3)
    F(1)
    F(3)
    H(2)
    O(1)
    O(3)
    C(0, True)
    F(2)
    O(2)
    C(1)
    C(3)
    return_forward()
    C(2)

    block = tokens // RING
    sub = block // RING
    cols = width // 2
    near_r, near_l, near_rr, near_ll = dev_z(1), dev_z(-1), dev_z(2), dev_z(-2)
    far_devs = (dev_z(4), dev_z(-4), dev_z(8))
    streams = [zbufs[6 * q:6 * q + 6] for q in range(2)]
    ks_near, ks_sum, ks_far, ks_out = [[take(n) for _ in range(2)] for n in (4, 3, 3, 3 * RING)]

    def ring(i, j):
        return lax.rem(i + RING + j, RING)

    for q, (mine, one, two, mid, far_in, done) in enumerate(streams):
        mine[...] = acc[:, q * cols:(q + 1) * cols].astype(BF).reshape(mine.shape)
        k = ks_near[q]
        send(mine.at[ring(za, 2), 0], two.at[0], near_rr, k + 2, k + 2)
        send(mine.at[ring(za, 2), 1], two.at[1], near_ll, k + 3, k + 3)
        send(mine.at[ring(za, 1)], one.at[0], near_r, k, k)
        send(mine.at[ring(za, -1)], one.at[1], near_l, k + 1, k + 1)
    pl.semaphore_wait(ready, 2)
    for q, (mine, one, two, mid, far_in, done) in enumerate(streams):
        k = ks_near[q]
        for n in (0, 1):
            arrived(two.at[n], k + 2 + n)
            arrived(one.at[n], k + n)
        total = mine[za].astype(F32) + one[0].astype(F32) + one[1].astype(F32) + two[...].astype(F32)
        mid[...] = total.astype(BF).reshape(mid.shape)
        for n in (2, 0, 1):
            send(mid.at[ring(zb, (1, -1, 2)[n])], far_in.at[n], far_devs[n], ks_sum[q] + n, ks_sum[q] + n)

    def spread(q, b):
        done = streams[q][5]
        k = ks_out[q] + 3 * b
        ref = done.at[za, b]
        send(ref, ref, near_r, k, k)
        send(ref, ref, near_l, k + 1, k + 1)
        send(ref, ref, dev_z(2 - 4 * lax.div(b, 2)), k + 2, k + 2)

    for q, (mine, one, two, mid, far_in, done) in enumerate(streams):
        for n in (0, 1, 2):
            arrived(far_in.at[n], ks_sum[q] + n)
        total = mid[zb].astype(F32) + far_in[0].astype(F32) + far_in[1].astype(F32) + far_in[2].astype(F32)
        done[za, zb] = total.astype(BF)
        for n in (2, 0, 1):
            send(done.at[za, zb], done.at[za, zb], far_devs[n], ks_far[q] + n, ks_far[q] + n)
        spread(q, zb)
    for n in (0, 1, 2):
        for q in range(2):
            b = ring(zb, (-1, 1, 2)[n])
            arrived(streams[q][5].at[za, b], ks_far[q] + n)
            spread(q, b)
    for q in range(2):
        done = streams[q][5]
        for b in range(RING):
            for n, j in enumerate((-1, 1, 2)):
                arrived(done.at[ring(za, j), b], ks_out[q] + 3 * b + n)
        out[:, q * cols:(q + 1) * cols] = done[...].reshape(tokens, cols)
    for copy in pending:
        copy.wait_send()


def local(tokens, route_ids, gates, w_gate, w_up, w_down):
    w_gate, w_up, w_down = w_gate[0], w_up[0], w_down[0]
    n, width = tokens.shape
    units = w_gate.shape[1]
    block = n // RING
    sub = block // RING
    V = pltpu.VMEM
    zbufs = []
    for _ in range(2):
        cols = width // 2
        zbufs += [V((RING, 2, block // 2, cols), BF), V((2, 2, block // 2, cols), BF),
                  V((2, block // 2, cols), BF), V((RING, sub, cols), BF),
                  V((3, sub, cols), BF), V((RING, RING, sub, cols), BF)]
    scratch = [
        V(tokens.shape, BF), V(w_gate.shape, BF), V(w_up.shape, BF), V(w_down.shape, BF),
        V((16, n), F32),
        V((128, n), F32),
        V((RING, 2, CAP, width), BF),
        V((RING, 2, CAP, width), BF),
        V((2, QUARTER, width), BF),
        V((RING, 2, QUARTER, width), BF),
        V((RING, 2, RING, PART, units), BF),
        V((RING, 2, PART, units), BF),
        V((RING, 4, PART, units), BF),
        V((RING, 2, PART, units), BF),
        V((RING, 2, RING, PART, units // 2), BF),
        V((RING, 2, CAP, width), BF),
        V((RING, 2, QUARTER, width), BF),
        V((2, 2, 2, QUARTER, width), BF),
        V((RING, 2, CAP, width), BF),
        V((2, RING, QUARTER, width), BF),
        V((RING, n, ROWS), BF),
        V((n, width), F32),
        *zbufs,
        pltpu.SemaphoreType.DMA((4,)),
        pltpu.SemaphoreType.DMA((NSEM,)),
        pltpu.SemaphoreType.DMA((NSEM,)),
        pltpu.SemaphoreType.REGULAR,
    ]
    vmem = pl.BlockSpec(memory_space=pltpu.VMEM)
    hbm = pl.BlockSpec(memory_space=pltpu.HBM)
    return pl.pallas_call(
        kernel,
        out_shape=jax.ShapeDtypeStruct((n, width), BF),
        in_specs=[hbm, vmem, vmem, hbm, hbm, hbm],
        out_specs=vmem,
        scratch_shapes=scratch,
        compiler_params=pltpu.CompilerParams(
            collective_id=0, has_side_effects=True, vmem_limit_bytes=66400000),
        name="expert_layer",
    )(tokens, route_ids.T, gates.T, w_gate, w_up, w_down)


def solution(mesh):
    return jax.shard_map(
        local,
        mesh=mesh,
        in_specs=(
            P("expert", "dp"),
            P("expert", None),
            P("expert", None),
            P("expert", "dp", "tensor"),
            P("expert", "dp", "tensor"),
            P("expert", "tensor", "dp"),
        ),
        out_specs=P("expert", "dp"),
        check_vma=False,
    )
```

time: 103 us -> 89.3 us (0.87)
  the two profiles are of different devices: /device:TPU:46 before, /device:TPU:2 now
where the time goes in v2:
time: 89.3 us; the launch traced here: 89.1 us
  Pallas kernels  87.3 us (98%)
  local copies, waits for them, and re-layouts  1.77 us (2%)
    pallas_call x1, Pallas kernels, local(): pl.pallas_call(kernel, out_shape=jax.ShapeDtypeStruct((n, width), BF), in...  87.3 us

profile of v2, /device:TPU:2, one launch (start us, length us, event | category | flops | bytes accessed | tf_op | source)
XLA Modules:
  0.0 89.1 jit_solution(17372904153556082628)
XLA Ops:
  0.0 87.3 %expert_layer.1 = bf16[256,768]{1,0:T(8,128)(2,1)} custom-call(bf16[256,768]{1,0:T(8,128)(2,1)} %tok_h.1, s32[2,256]{1,0:T(2,128)} %bitcast.8, f32[2,256]{1,0:T(2,128)} %bitcast.9, bf16[768,512]{1,0:T(8,128)(2,1)} %bitcast.5, bf16[768,512]{1,0:T(8,128)(2,1)} %bitcast.6, bf16[512,768]{1,0:T(8,128)(2,1)} %bitcast.7), custom_call_target="tpu_custom_call" | custom-call | tf_op jit(solution)/shard_map/expert_layer/pallas_call | solution.py:422
  87.3 1.8 %copy.8 = bf16[256,768]{1,0:T(8,128)(2,1)} copy(bf16[256,768]{1,0:T(8,128)(2,1)} %expert_layer.1) | data formatting | bytes 786432

commit v3 on v2

--- a/solution.py
+++ b/solution.py
@@ -16,8 +16,8 @@
 QUARTER = CAP // RING
 
 
-def kernel(tok_h, route, gates, wg_h, wu_h, wd_h, out, *s):
-    (tok, wg, wu, wd, slots, table, pick, rows, farpick, far_rows, part, rl, fin, cmb, hid, obuf, far_out, rhop, ret,
+def kernel(tok_h, route_h, gates_h, wg_h, wu_h, wd_h, out, *s):
+    (route, gates, tok, wg, wu, wd, slots, table, pick, rows, farpick, far_rows, part, rl, fin, cmb, hid, obuf, far_out, rhop, ret,
      far_ret, gm, acc, *zbufs) = s[:-4]
     wsem, ssem, rsem, ready = s[-4:]
     tokens, width = tok.shape
@@ -40,13 +40,14 @@
         return {"tensor": lax.rem(z + nz + j, nz)}
 
     loads = [pltpu.make_async_copy(a, b, wsem.at[i])
-             for i, (a, b) in enumerate(((tok_h, tok), (wg_h, wg), (wu_h, wu), (wd_h, wd)))]
+             for i, (a, b) in enumerate(((route_h, route), (gates_h, gates), (tok_h, tok), (wg_h, wg),
+                                    (wu_h, wu), (wd_h, wd)))]
     for load in loads:
         load.start()
 
     barrier = pltpu.get_barrier_semaphore()
     peers = [dev_e(0, 1 - c)] + [dev_e(j, k) for j in (1, 2, 3) for k in (0, 1)]
-    peers += [dev_x(1), dev_x(3)] + [dev_z(j) for j in (1, -1, 2, -2, 4, -4)]
+    peers += [dev_x(1), dev_x(3)] + [dev_z(j) for j in (1, -1, 2, -2)]
     for peer in peers:
         pl.semaphore_signal(barrier, inc=1, device_id=peer, device_id_type=pl.DeviceIdType.MESH)
 
@@ -71,6 +72,8 @@
             src_ref=dst, dst_ref=dst, send_sem=ssem.at[0], recv_sem=rsem.at[k],
             device_id=dev_e(0, 1 - c), device_id_type=pl.DeviceIdType.MESH).wait_recv()
 
+    loads[0].wait()
+    loads[1].wait()
     r0, r1 = route[0:1, :], route[1:2, :]
     line = lax.broadcasted_iota(jnp.int32, (16, tokens), 0)
     hit0, hit1 = line == r0, line == r1
@@ -100,25 +103,29 @@
     k_own = take()
     za, zb = lax.rem(z, RING), lax.div(z, RING)
 
-    loads[0].wait()
+    loads[2].wait()
     line = lax.broadcasted_iota(jnp.int32, (2 * QUARTER, tokens), 0)
     slot = jnp.where(line < QUARTER, line, line - QUARTER) + za * QUARTER
     place = jnp.where(line < QUARTER, slots[pl.ds(chip(2) * 2, 1), :], slots[pl.ds(chip(2) * 2 + 1, 1), :])
     chosen = jnp.where(slot.astype(F32) == place, 1.0, 0.0).astype(BF)
     got = jnp.dot(chosen, tok[...], preferred_element_type=F32).astype(BF)
     farpick[...] = got.reshape(2, QUARTER, width)
+    for j in (3, 1, 0):
+        picked(j)
     pl.semaphore_wait(barrier, len(peers))
     for core in (0, 1):
         send(farpick.at[core], far_rows.at[za, c], dev_e(2, core), k_far + core, k_far + c)
-    for j in (4, -4):
-        pl.semaphore_signal(ready, inc=1, device_id=dev_z(j), device_id_type=pl.DeviceIdType.MESH)
     for j in (3, 1):
-        picked(j)
         for core in (0, 1):
             send(pick.at[j, core], rows.at[RING - j, c], dev_e(j, core), ks_d[j] + core, ks_d[j] + c)
-    picked(0)
     send(pick.at[0, 1 - c], rows.at[0, c], dev_e(0, 1 - c), k_own, k_own)
     rows[0, c] = pick[0, c]
+
+    def vouch(n, hops):
+        for j in (hops, -hops):
+            pl.semaphore_signal(ready.at[n], inc=1, device_id=dev_z(j), device_id_type=pl.DeviceIdType.MESH)
+
+    vouch(0, 2)
 
     def far_spread():
         for core in (0, 1):
@@ -206,8 +213,8 @@
     def G(j):
         rows_here(j)
         if j == 0:
-            loads[1].wait()
-            loads[2].wait()
+            loads[3].wait()
+            loads[4].wait()
         here = (far_rows if j == 2 else rows.at[j])[...].reshape(ROWS, width)
         for n, w in enumerate((wg, wu)):
             got = jnp.dot(here, w[...], preferred_element_type=F32).astype(BF)
@@ -230,22 +237,24 @@
 
     k_ret = {j: take(2) for j in (1, 3)}
     k_rhop = take(4)
-    k_rfwd = {1: take(4), 3: take(4)}
+    k_rfwd = take(8)
+    cols = width // 2
     k_rown = take()
 
     def O(j, first_use=False):
         ag_finish(ag_k[j], hid_at(j), x)
         if first_use:
-            loads[3].wait()
+            loads[5].wait()
         hw = wd.shape[0] // 2
         got = jnp.dot(hid[j, 0].reshape(ROWS, hw), wd[0:hw], preferred_element_type=F32)
         got += jnp.dot(hid[j, 1].reshape(ROWS, hw), wd[hw:], preferred_element_type=F32)
         got = got.astype(BF)
         if j == 2:
-            far_out[...] = got.reshape(far_out.shape)
-            for a in (0, 1):
+            for q in (0, 1):
+                far_out[q] = got[:, q * cols:(q + 1) * cols].reshape(far_out.shape[1:])
                 for n in (0, 1):
-                    send(far_out.at[2 * n + a], rhop.at[n, a], dev_e(1 + 2 * n, c), k_rhop + 2 * n + a, k_rhop + 2 * n + a)
+                    k = k_rhop + 2 * q + n
+                    send(far_out.at[q, 2 * n:2 * n + 2], rhop.at[q, n], dev_e(1 + 2 * n, c), k, k)
             return
         obuf[j] = got.reshape(2, CAP, width)
         if j == 0:
@@ -255,13 +264,12 @@
             for core in (0, 1):
                 send(obuf.at[j, core], ret.at[RING - j, c], dev_e(j, core), k_ret[j] + core, k_ret[j] + c)
 
-    def return_forward():
-        for a in (0, 1):
-            for n in (0, 1):
-                arrived(rhop.at[n, a], k_rhop + 2 * n + a)
-                k = k_rfwd[1 + 2 * n] + 2 * a
-                for core in (0, 1):
-                    send(rhop.at[n, a, core], far_ret.at[c, 2 * n + a], dev_e(1 + 2 * n, core), k + core, k + c)
+    def return_forward(q):
+        for n in (0, 1):
+            arrived(rhop.at[q, n], k_rhop + 2 * q + n)
+            k = k_rfwd + 4 * q + 2 * n
+            for core in (0, 1):
+                send(rhop.at[q, n, :, core], far_ret.at[q, c, 2 * n:2 * n + 2], dev_e(1 + 2 * n, core), k + core, k + c)
 
     def combine_table():
         by_token = table[...].T
@@ -275,16 +283,10 @@
     def C(j, first=False):
         if j == 0:
             arrived(ret.at[0, 1 - c], k_rown)
-        elif j == 2:
-            for a in (0, 1):
-                for n in (0, 1):
-                    for core in (0, 1):
-                        arrived(far_ret.at[core, 2 * n + a], k_rfwd[1 + 2 * n] + 2 * a + core)
         else:
             for core in (0, 1):
                 arrived(ret.at[j, core], k_ret[RING - j] + core)
-        back = (far_ret if j == 2 else ret.at[j])[...].reshape(ROWS, width)
-        got = jnp.dot(gm[j], back, preferred_element_type=F32)
+        got = jnp.dot(gm[j], ret[j].reshape(ROWS, width), preferred_element_type=F32)
         if first:
             acc[...] = got
         else:
@@ -292,6 +294,8 @@
 
     G(0)
     combine_table()
+    pl.semaphore_wait(ready.at[0], 2)
+    vouch(1, 4)
     R(0)
     far_spread()
     H(0)
@@ -315,12 +319,11 @@
     O(2)
     C(1)
     C(3)
-    return_forward()
-    C(2)
+    return_forward(0)
+    return_forward(1)
 
     block = tokens // RING
     sub = block // RING
-    cols = width // 2
     near_r, near_l, near_rr, near_ll = dev_z(1), dev_z(-1), dev_z(2), dev_z(-2)
     far_devs = (dev_z(4), dev_z(-4), dev_z(8))
     streams = [zbufs[6 * q:6 * q + 6] for q in range(2)]
@@ -330,13 +333,17 @@
         return lax.rem(i + RING + j, RING)
 
     for q, (mine, one, two, mid, far_in, done) in enumerate(streams):
-        mine[...] = acc[:, q * cols:(q + 1) * cols].astype(BF).reshape(mine.shape)
+        for n in (0, 1):
+            for core in (0, 1):
+                arrived(far_ret.at[q, core, 2 * n:2 * n + 2], k_rfwd + 4 * q + 2 * n + core)
+        got = jnp.dot(gm[2], far_ret[q].reshape(ROWS, cols), preferred_element_type=F32)
+        mine[...] = (acc[:, q * cols:(q + 1) * cols] + got).astype(BF).reshape(mine.shape)
         k = ks_near[q]
         send(mine.at[ring(za, 2), 0], two.at[0], near_rr, k + 2, k + 2)
         send(mine.at[ring(za, 2), 1], two.at[1], near_ll, k + 3, k + 3)
         send(mine.at[ring(za, 1)], one.at[0], near_r, k, k)
         send(mine.at[ring(za, -1)], one.at[1], near_l, k + 1, k + 1)
-    pl.semaphore_wait(ready, 2)
+    pl.semaphore_wait(ready.at[1], 2)
     for q, (mine, one, two, mid, far_in, done) in enumerate(streams):
         k = ks_near[q]
         for n in (0, 1):
@@ -392,6 +399,7 @@
                   V((2, block // 2, cols), BF), V((RING, sub, cols), BF),
                   V((3, sub, cols), BF), V((RING, RING, sub, cols), BF)]
     scratch = [
+        V((2, n), jnp.int32), V((2, n), F32),
         V(tokens.shape, BF), V(w_gate.shape, BF), V(w_up.shape, BF), V(w_down.shape, BF),
         V((16, n), F32),
         V((128, n), F32),
@@ -405,30 +413,31 @@
         V((RING, 2, PART, units), BF),
         V((RING, 2, RING, PART, units // 2), BF),
         V((RING, 2, CAP, width), BF),
-        V((RING, 2, QUARTER, width), BF),
-        V((2, 2, 2, QUARTER, width), BF),
+        V((2, RING, 2, QUARTER, width // 2), BF),
+        V((2, 2, 2, 2, QUARTER, width // 2), BF),
         V((RING, 2, CAP, width), BF),
-        V((2, RING, QUARTER, width), BF),
+        V((2, 2, RING, QUARTER, width // 2), BF),
         V((RING, n, ROWS), BF),
         V((n, width), F32),
         *zbufs,
-        pltpu.SemaphoreType.DMA((4,)),
+        pltpu.SemaphoreType.DMA((6,)),
         pltpu.SemaphoreType.DMA((NSEM,)),
         pltpu.SemaphoreType.DMA((NSEM,)),
-        pltpu.SemaphoreType.REGULAR,
+        pltpu.SemaphoreType.REGULAR((2,)),
     ]
     vmem = pl.BlockSpec(memory_space=pltpu.VMEM)
     hbm = pl.BlockSpec(memory_space=pltpu.HBM)
     return pl.pallas_call(
         kernel,
         out_shape=jax.ShapeDtypeStruct((n, width), BF),
-        in_specs=[hbm, vmem, vmem, hbm, hbm, hbm],
+        in_specs=[hbm] * 6,
         out_specs=vmem,
         scratch_shapes=scratch,
         compiler_params=pltpu.CompilerParams(
-            collective_id=0, has_side_effects=True, vmem_limit_bytes=66400000),
+            collective_id=0, has_side_effects=True, vmem_limit_bytes=40 * 1024 * 1024),
         name="expert_layer",
-    )(tokens, route_ids.T, gates.T, w_gate, w_up, w_down)
+    )(*[pltpu.with_memory_space_constraint(v, pltpu.HBM)
+        for v in (tokens, route_ids.T, gates.T, w_gate, w_up, w_down)])
 
 
 def solution(mesh):

time: 89.3 us -> 84.7 us (0.948)
  the two profiles are of different devices: /device:TPU:2 before, /device:TPU:8 now
where the time goes in v3:
time: 84.7 us; the launch traced here: 84.6 us
  Pallas kernels  83.8 us (99%)
    pallas_call x1, Pallas kernels, local(): pl.pallas_call(kernel, out_shape=jax.ShapeDtypeStruct((n, width), BF), in...  83.8 us

profile of v3, /device:TPU:8, one launch (start us, length us, event | category | flops | bytes accessed | tf_op | source)
XLA Modules:
  0.0 84.6 jit_solution(1642899759649967078)
XLA Ops:
  0.0 83.8 %expert_layer.1 = bf16[256,768]{1,0:T(8,128)(2,1)S(1)} custom-call(bf16[256,768]{1,0:T(8,128)(2,1)} %tok_h.1, s32[2,256]{1,0:T(2,128)} %bitcast.8, f32[2,256]{1,0:T(2,128)} %bitcast.9, bf16[768,512]{1,0:T(8,128)(2,1)} %bitcast.5, bf16[768,512]{1,0:T(8,128)(2,1)} %bitcast.6, bf16[512,768]{1,0:T(8,128)(2,1)} %bitcast.7), custom_call_target="tpu_custom_call" | custom-call | tf_op jit(solution)/shard_map/expert_layer/pallas_call | solution.py:430
  83.8 0.7 copy.8

commit v4 on v3

--- a/solution.py
+++ b/solution.py
@@ -14,10 +14,12 @@
 NONE = -1000.0
 NSEM = 190
 QUARTER = CAP // RING
+ROUTED_SUM = (2,)
+ROUTED_GATHER = (2,)
 
 
 def kernel(tok_h, route_h, gates_h, wg_h, wu_h, wd_h, out, *s):
-    (route, gates, tok, wg, wu, wd, slots, table, pick, rows, farpick, far_rows, part, rl, fin, cmb, hid, obuf, far_out, rhop, ret,
+    (route, gates, tok, wg, wu, wd, slots, table, pick, rows, farpick, far_rows, part, rl, fin, cmb, hid, obuf, far_out, ret,
      far_ret, gm, acc, *zbufs) = s[:-4]
     wsem, ssem, rsem, ready = s[-4:]
     tokens, width = tok.shape
@@ -47,7 +49,7 @@
 
     barrier = pltpu.get_barrier_semaphore()
     peers = [dev_e(0, 1 - c)] + [dev_e(j, k) for j in (1, 2, 3) for k in (0, 1)]
-    peers += [dev_x(1), dev_x(3)] + [dev_z(j) for j in (1, -1, 2, -2)]
+    peers += [dev_x(1), dev_x(2), dev_x(3)] + [dev_z(j) for j in (1, -1, 2, -2)]
     for peer in peers:
         pl.semaphore_signal(barrier, inc=1, device_id=peer, device_id_type=pl.DeviceIdType.MESH)
 
@@ -175,6 +177,18 @@
         second = own[1][i].astype(F32) + done[0][...].astype(F32) + done[3][...].astype(F32)
         return first, second
 
+    def rs_routed(own, i, left, right, across, bufs):
+        k = take(6)
+        relay, done, _ = bufs
+        opp, r, l = lax.rem(i + 2, RING), lax.rem(i + 1, RING), lax.rem(i + 3, RING)
+        send(own[0].at[opp], relay[0], across, k, k)
+        send(own[1].at[opp], relay[1], across, k + 1, k + 1)
+        send(own[1].at[r], done[0], right, k + 2, k + 2)
+        send(own[0].at[l], done[1], left, k + 3, k + 3)
+        send(own[0].at[r], done[2], right, k + 4, k + 4)
+        send(own[1].at[l], done[3], left, k + 5, k + 5)
+        return k
+
     def ag_start(at, i, left, right):
         k = take(6)
         send(at(0, i), at(0, i), right, k, k)
@@ -183,6 +197,16 @@
         send(at(0, i), at(0, i), left, k + 3, k + 3)
         return k
 
+    def ag_routed(at, i, left, right, across):
+        k = take(6)
+        send(at(0, i), at(0, i), across, k + 4, k + 4)
+        send(at(1, i), at(1, i), across, k + 5, k + 5)
+        send(at(0, i), at(0, i), right, k, k)
+        send(at(1, i), at(1, i), left, k + 1, k + 1)
+        send(at(1, i), at(1, i), right, k + 2, k + 2)
+        send(at(0, i), at(0, i), left, k + 3, k + 3)
+        return k
+
     def ag_relay(k, at, i, left, right):
         r, l = lax.rem(i + 1, RING), lax.rem(i + 3, RING)
         arrived(at(0, l), k)
@@ -197,7 +221,7 @@
         arrived(at(0, opp), k + 4)
         arrived(at(1, opp), k + 5)
 
-    xl, xr = dev_x(3), dev_x(1)
+    xl, xr, xo = dev_x(3), dev_x(1), dev_x(2)
     rs_k, ag_k = {}, {}
 
     def xbufs(j):
@@ -219,29 +243,44 @@
         for n, w in enumerate((wg, wu)):
             got = jnp.dot(here, w[...], preferred_element_type=F32).astype(BF)
             part[j, n] = got.reshape(RING, PART, got.shape[1])
-        rs_k[j] = rs_start(xown(j), x, xl, xr, xbufs(j))
+        if j in ROUTED_SUM:
+            rs_k[j] = rs_routed(xown(j), x, xl, xr, xo, xbufs(j))
+        else:
+            rs_k[j] = rs_start(xown(j), x, xl, xr, xbufs(j))
 
     def R(j):
-        rs_relay(rs_k[j], xown(j), x, xl, xr, xbufs(j))
+        if j not in ROUTED_SUM:
+            rs_relay(rs_k[j], xown(j), x, xl, xr, xbufs(j))
 
     def H(j):
         gate, up = rs_finish(rs_k[j], xown(j), x, xbufs(j))
+        if j in ROUTED_SUM:
+            for n in range(2):
+                arrived(rl.at[j, n], rs_k[j] + n)
+            gate += rl[j, 0].astype(F32)
+            up += rl[j, 1].astype(F32)
         got = (gate / (1.0 + jnp.exp(-gate)) * up).astype(BF)
         hw = got.shape[1] // 2
         hid[j, 0, x] = got[:, :hw]
         hid[j, 1, x] = got[:, hw:]
-        ag_k[j] = ag_start(hid_at(j), x, xl, xr)
+        if j in ROUTED_GATHER:
+            ag_k[j] = ag_routed(hid_at(j), x, xl, xr, xo)
+        else:
+            ag_k[j] = ag_start(hid_at(j), x, xl, xr)
 
     def F(j):
-        ag_relay(ag_k[j], hid_at(j), x, xl, xr)
+        if j not in ROUTED_GATHER:
+            ag_relay(ag_k[j], hid_at(j), x, xl, xr)
 
     k_ret = {j: take(2) for j in (1, 3)}
-    k_rhop = take(4)
-    k_rfwd = take(8)
+    k_rfar = take(4)
     cols = width // 2
     k_rown = take()
 
     def O(j, first_use=False):
+        if j in ROUTED_GATHER:
+            arrived(hid_at(j)(0, lax.rem(x + 3, RING)), ag_k[j])
+            arrived(hid_at(j)(1, lax.rem(x + 1, RING)), ag_k[j] + 1)
         ag_finish(ag_k[j], hid_at(j), x)
         if first_use:
             loads[5].wait()
@@ -252,9 +291,8 @@
         if j == 2:
             for q in (0, 1):
                 far_out[q] = got[:, q * cols:(q + 1) * cols].reshape(far_out.shape[1:])
-                for n in (0, 1):
-                    k = k_rhop + 2 * q + n
-                    send(far_out.at[q, 2 * n:2 * n + 2], rhop.at[q, n], dev_e(1 + 2 * n, c), k, k)
+                for core in (0, 1):
+                    send(far_out.at[q, :, core], far_ret.at[q, c], dev_e(2, core), k_rfar + 2 * q + core, k_rfar + 2 * q + c)
             return
         obuf[j] = got.reshape(2, CAP, width)
         if j == 0:
@@ -263,13 +301,6 @@
         else:
             for core in (0, 1):
                 send(obuf.at[j, core], ret.at[RING - j, c], dev_e(j, core), k_ret[j] + core, k_ret[j] + c)
-
-    def return_forward(q):
-        for n in (0, 1):
-            arrived(rhop.at[q, n], k_rhop + 2 * q + n)
-            k = k_rfwd + 4 * q + 2 * n
-            for core in (0, 1):
-                send(rhop.at[q, n, :, core], far_ret.at[q, c, 2 * n:2 * n + 2], dev_e(1 + 2 * n, core), k + core, k + c)
 
     def combine_table():
         by_token = table[...].T
@@ -319,8 +350,6 @@
     O(2)
     C(1)
     C(3)
-    return_forward(0)
-    return_forward(1)
 
     block = tokens // RING
     sub = block // RING
@@ -333,9 +362,8 @@
         return lax.rem(i + RING + j, RING)
 
     for q, (mine, one, two, mid, far_in, done) in enumerate(streams):
-        for n in (0, 1):
-            for core in (0, 1):
-                arrived(far_ret.at[q, core, 2 * n:2 * n + 2], k_rfwd + 4 * q + 2 * n + core)
+        for core in (0, 1):
+            arrived(far_ret.at[q, core], k_rfar + 2 * q + core)
         got = jnp.dot(gm[2], far_ret[q].reshape(ROWS, cols), preferred_element_type=F32)
         mine[...] = (acc[:, q * cols:(q + 1) * cols] + got).astype(BF).reshape(mine.shape)
         k = ks_near[q]
@@ -414,7 +442,6 @@
         V((RING, 2, RING, PART, units // 2), BF),
         V((RING, 2, CAP, width), BF),
         V((2, RING, 2, QUARTER, width // 2), BF),
-        V((2, 2, 2, 2, QUARTER, width // 2), BF),
         V((RING, 2, CAP, width), BF),
         V((2, 2, RING, QUARTER, width // 2), BF),
         V((RING, n, ROWS), BF),

time: 84.7 us -> 83.3 us (0.983)
  the two profiles are of different devices: /device:TPU:8 before, /device:TPU:2 now
where the time goes in v4:
time: 83.3 us; the launch traced here: 83.2 us
  Pallas kernels  82.4 us (99%)
    pallas_call x1, Pallas kernels, local(): pl.pallas_call(kernel, out_shape=jax.ShapeDtypeStruct((n, width), BF), in...  82.4 us

profile of v4, /device:TPU:2, one launch (start us, length us, event | category | flops | bytes accessed | tf_op | source)
XLA Modules:
  0.0 83.2 jit_solution(10717740576903070859)
XLA Ops:
  0.0 82.4 %expert_layer.1 = bf16[256,768]{1,0:T(8,128)(2,1)S(1)} custom-call(bf16[256,768]{1,0:T(8,128)(2,1)} %tok_h.1, s32[2,256]{1,0:T(2,128)} %bitcast.8, f32[2,256]{1,0:T(2,128)} %bitcast.9, bf16[768,512]{1,0:T(8,128)(2,1)} %bitcast.5, bf16[768,512]{1,0:T(8,128)(2,1)} %bitcast.6, bf16[512,768]{1,0:T(8,128)(2,1)} %bitcast.7), custom_call_target="tpu_custom_call" | custom-call | tf_op jit(solution)/shard_map/expert_layer/pallas_call | solution.py:457
  82.4 0.7 copy.8
